TPU v7x, 32 devices: a whole 2x2x4 slice. The times are simulated.
32 devices in a mesh: req: 4 (over y, core), seq: 8 (over z, x).
Axes of the slice: x: 2, y: 2, z: 4, core: 2. Of those that a mesh axis runs over, the one named last changes fastest.
Arguments:
- embedded: bfloat16 [4, 48, 3584], P(None, 'req'), may hold values from -6 to 6
- cache_keys: bfloat16 [4, 4096, 2048], P('req', 'seq'), may hold values from -6 to 6
- cache_values: bfloat16 [4, 4096, 2048], P('req', 'seq'), may hold values from -6 to 6
- token_owner: int32 [4, 4096], P('req', 'seq'), may hold values from 0 to 11, as said below
- dealing: int32 [48], replicated, may hold values from 0 to 47, as said below
- lengths: int32 [48], replicated, may hold values from 1 to 2048, as said below
- project_weight: bfloat16 [3584, 8192], P(None, 'seq')
- output_weight: bfloat16 [4096, 3584], P('seq'), may hold values from -0.09375 to 0.09375
- gate_weight: bfloat16 [3584, 14336], P(None, ('req', 'seq')), may hold values from -0.09375 to 0.09375
- up_weight: bfloat16 [3584, 14336], P(None, ('req', 'seq')), may hold values from -0.09375 to 0.09375
- down_weight: bfloat16 [14336, 3584], P(('req', 'seq')), may hold values from -0.046875 to 0.046875
- gain_first: float32 [3584], replicated, may hold values from 0.1 to 1.9
- gain_second: float32 [3584], replicated, may hold values from 0.1 to 1.9
- gain_third: float32 [3584], replicated, may hold values from 0.1 to 1.9
- gain_fourth: float32 [3584], replicated, may hold values from 0.1 to 1.9
Outputs:
- results: bfloat16 [4, 48, 3584], P(None, 'req')
Inputs may be any that keep to these rules, and one draw needn't show every extreme that they name: A permutation of the requests; slot i of req group g serves request dealing[g * 12 + i]. The lengths of the 12 requests dealt to one group sum to 4096; in every group the longest is exactly 2048. `token_owner`: each slot owns a contiguous run of its group's pool, runs in slot order, as many tokens as its request's length.
All inputs are finite; a program needn't handle non-finite values.
Results may differ from a plain program's by a relative error of at most 0.012.
The roundings to bfloat16 on the way count: a program that leaves them out, or rounds other values in their place, can miss the bound.
Values may be sent and summed in bfloat16 or wider, within the bound.
A program may use at most 128 MiB of HBM per device.

v0:
```python
import math
import jax
import jax.numpy as jnp
from jax import lax
from jax.sharding import PartitionSpec as P

H = 16
KVH = 8
HD = 256
STEPS = 4
soft_cap = 50.0
epsilon = 1e-06


def rms_scale(values, gain):
    mean_square = jnp.mean(values * values, axis=-1, keepdims=True)
    return values * lax.rsqrt(mean_square + epsilon) * gain


def rotate(values, positions):
    half_width = values.shape[-1] // 2
    freq_index = jnp.arange(half_width, dtype=jnp.float32)
    inverse = jnp.exp(freq_index * (-2.0 * math.log(10000.0) / values.shape[-1]))
    angles = positions[:, None] * inverse[None, :]
    cosine = jnp.cos(angles)[:, None, :]
    sine = jnp.sin(angles)[:, None, :]
    first_half = values[..., :half_width]
    second_half = values[..., half_width:]
    return jnp.concatenate(
        [first_half * cosine - second_half * sine, second_half * cosine + first_half * sine],
        axis=-1,
    )


def capped_weight(scores):
    return jnp.exp(soft_cap * jnp.tanh(scores / soft_cap))


def rounded(values):
    return lax.optimization_barrier(values.astype(jnp.bfloat16)).astype(jnp.float32)


def body(
    embedded,
    cache_keys,
    cache_values,
    token_owner,
    dealing,
    lengths,
    project_weight,
    output_weight,
    gate_weight,
    up_weight,
    down_weight,
    gain_first,
    gain_second,
    gain_third,
    gain_fourth,
):
    row_count = embedded.shape[1]
    rows = STEPS * row_count
    width = embedded.shape[2]
    local_tokens = cache_keys.shape[1]
    value_width = cache_keys.shape[2]
    group_size = H // KVH
    attention_width = H * HD
    column_count = output_weight.shape[0]
    group_index = lax.axis_index("req")
    seq_index = lax.axis_index("seq")
    seq_size = lax.axis_size("seq")
    req_size = lax.axis_size("req")
    column_start = seq_index * column_count
    slot_requests = lax.dynamic_slice_in_dim(dealing, group_index * row_count, row_count)
    matches = slot_requests[:, None] == jnp.arange(dealing.shape[0], dtype=jnp.int32)[None, :]
    base_positions = jnp.sum(jnp.where(matches, lengths[None, :], 0), axis=1)
    positions = base_positions[None, :] + jnp.arange(STEPS, dtype=jnp.int32)[:, None]
    positions = positions.reshape(rows).astype(jnp.float32)
    key_pool = cache_keys[0].reshape(local_tokens, KVH, HD)
    value_pool = cache_values[0].reshape(local_tokens, KVH, HD)
    slots = jnp.tile(jnp.arange(row_count, dtype=jnp.int32), STEPS)
    moments = jnp.repeat(jnp.arange(STEPS, dtype=jnp.int32), row_count)
    owned_mask = token_owner[0][None, :] == slots[:, None]
    stream = embedded.reshape(rows, width).astype(jnp.float32)
    normed = rms_scale(stream, gain_first).astype(jnp.bfloat16)
    local_part = jnp.dot(normed, project_weight, preferred_element_type=jnp.float32).astype(
        jnp.bfloat16
    )
    projected = lax.all_gather(local_part, "seq", axis=1, tiled=True)
    query_rows = projected[:, :attention_width].astype(jnp.float32).reshape(rows, H, HD)
    queries = (rotate(query_rows, positions) * HD ** (-0.5)).astype(jnp.bfloat16)
    key_rows = (
        projected[:, attention_width : attention_width + value_width]
        .astype(jnp.float32)
        .reshape(rows, KVH, HD)
    )
    fresh_keys = rotate(key_rows, positions).astype(jnp.bfloat16)
    fresh_values = projected[:, attention_width + value_width :].reshape(rows, KVH, HD)
    grouped = queries.reshape(rows, KVH, group_size, HD)
    all_keys = jnp.concatenate([key_pool, fresh_keys], axis=0)
    all_values = jnp.concatenate([value_pool, fresh_values], axis=0)
    fresh_mask = (
        (slots[None, :] == slots[:, None])
        & (moments[None, :] <= moments[:, None])
        & (seq_index == 0)
    )
    mask = jnp.concatenate([owned_mask, fresh_mask], axis=1)
    scores = jnp.einsum("igqd,tgd->igqt", grouped, all_keys, preferred_element_type=jnp.float32)
    weights = jnp.where(mask[:, None, None, :], capped_weight(scores), 0.0)
    totals = lax.psum(jnp.sum(weights, axis=-1), "seq").reshape(rows, H)
    outputs = jnp.einsum(
        "igqt,tgd->igqd",
        weights.astype(jnp.bfloat16),
        all_values,
        preferred_element_type=jnp.float32,
    ).reshape(rows, attention_width)
    outputs = lax.psum_scatter(outputs, "seq", scatter_dimension=1, tiled=True)
    spread = jnp.repeat(totals, HD, axis=1)
    spread = lax.dynamic_slice_in_dim(spread, column_start, column_count, 1)
    attended = (outputs / spread).astype(jnp.bfloat16)
    partial = jnp.dot(attended, output_weight, preferred_element_type=jnp.float32)
    mixed = lax.psum(partial, "seq")
    middle = stream + rms_scale(mixed, gain_second)
    feed_input = rms_scale(middle, gain_third).astype(jnp.bfloat16)
    block_rows = lax.all_gather(feed_input, "req", axis=0, tiled=True)
    gate_part = jnp.dot(block_rows, gate_weight, preferred_element_type=jnp.float32)
    up_part = jnp.dot(block_rows, up_weight, preferred_element_type=jnp.float32)
    hidden = (jax.nn.gelu(gate_part, approximate=True) * up_part).astype(jnp.bfloat16)
    summed = jnp.dot(hidden, down_weight, preferred_element_type=jnp.float32)
    summed = lax.psum_scatter(summed, "req", scatter_dimension=0, tiled=True)
    summed = lax.psum(summed, "seq")
    results = (middle + rms_scale(summed, gain_fourth)).astype(jnp.bfloat16)
    return results.reshape(STEPS, row_count, width)


def solution(mesh):
    return jax.shard_map(
        body,
        mesh=mesh,
        in_specs=(
            P(None, "req", None),
            P("req", "seq", None),
            P("req", "seq", None),
            P("req", "seq"),
            P(),
            P(),
            P(None, "seq"),
            P("seq", None),
            P(None, ("req", "seq")),
            P(None, ("req", "seq")),
            P(("req", "seq"), None),
            P(),
            P(),
            P(),
            P(),
        ),
        out_specs=P(None, "req", None),
        check_vma=False,
    )
```

profile of v0, /device:TPU:0, one launch (start us, length us, event | category | flops | bytes accessed | tf_op | source)
XLA Modules:
  0.0 383.3 jit_solution(17114336762805842567)
XLA Ops:
  6.6 2.1 copy.64
  8.7 1.2 multiply_reduce_fusion.3
  9.9 2.1 reshape.160
  12.2 4.8 %convolution_convert_fusion = bf16[48,1024]{1,0:T(8,128)(2,1)S(1)} fusion(bf16[3584,1024]{1,0:T(8,128)(2,1)} %param.21, f32[48,3584]{1,0:T(8,128)} %reshape.160, f32[3584]{0:T(1024)S(1)} %copy-done.4, f32[48]{0:T(128)S(1)} %rsqrt.36), kind=kOutput, calls=%fused_computation.14 | convolution fusion | flops 352886784 | bytes 8140992 | tf_op jit(solution)/shard_map/dot_general | solution.py:85
  17.0 33.8 %all_gather.6 = bf16[48,8192]{1,0:T(8,128)(2,1)S(1)} all-gather(bf16[48,1024]{1,0:T(8,128)(2,1)S(1)} %convolution_convert_fusion), channel_id=1, replica_groups=mesh['req'=4,'seq'=8] {'seq'}, dimensions={1}, use_global_device_ids=true | all-gather | bytes 884736 | tf_op jit(solution)/shard_map/all_gather | solution.py:88
  51.7 0.9 slice_convert_fusion
  53.1 1.1 copy.83
  54.9 1.4 copy.84
  58.6 3.9 %copy.69 = bf16[1,512,2048]{1,2,0:T(8,128)(2,1)} copy(bf16[1,512,2048]{2,1,0:T(8,128)(2,1)} %param.16) | data formatting | bytes 4194304 | tf_op args[1]
  62.6 3.9 %copy.72 = bf16[512,8,256]{2,0,1:T(8,128)(2,1)} copy(bf16[512,8,256]{0,2,1:T(8,128)(2,1)} %bitcast.44) | data formatting | bytes 4194304 | tf_op jit(solution)/shard_map/reshape;squeeze | solution.py:78
  66.5 1.6 copy.92
  68.1 3.9 %copy.65 = bf16[1,512,2048]{1,2,0:T(8,128)(2,1)} copy(bf16[1,512,2048]{2,1,0:T(8,128)(2,1)} %param.17) | data formatting | bytes 4194304 | tf_op args[2]
  72.0 3.9 %copy.67 = bf16[512,8,256]{2,0,1:T(8,128)(2,1)} copy(bf16[512,8,256]{0,2,1:T(8,128)(2,1)} %bitcast.45) | data formatting | bytes 4194304 | tf_op jit(solution)/shard_map/reshape;squeeze | solution.py:79
  76.0 1.0 subtract_convert_fusion
  77.0 2.9 fusion.40
  80.5 1.5 copy.75
  82.1 2.6 reshape.156
  84.8 21.7 %psum.21 = f32[48,16]{0,1:T(8,128)S(1)} all-reduce(f32[48,16]{0,1:T(8,128)S(1)} %bitcast.56), channel_id=1, replica_groups=mesh['req'=4,'seq'=8] {'seq'}, use_global_device_ids=true, to_apply=%region_4.5 | all-reduce | flops 768 | bytes 6144 | tf_op jit(solution)/shard_map/psum | solution.py:109
  106.7 1.4 copy.85
  108.1 40.9 %reduce-scatter.3.cloned.1.call-done = f32[48,512]{1,0:T(8,128)} async-done(((f32[48,4096]{1,0:T(8,128)}), f32[48,512]{1,0:T(8,128)}) %reduce-scatter.3.cloned.1.call-update) | async-done | bytes 98320 | tf_op jit(solution)/shard_map/reduce_scatter | solution.py:116
  149.0 3.8 fusion.29
  152.8 72.8 %all-reduce.3.cloned.1.call-done = f32[48,3584]{1,0:T(8,128)} async-done(((f32[48,3584]{1,0:T(8,128)}), f32[48,3584]{1,0:T(8,128)}) %all-reduce.3.cloned.1.call-update) | async-done | bytes 688144 | tf_op jit(solution)/shard_map/psum | solution.py:121
  225.6 1.2 multiply_reduce_fusion.2
  226.9 1.6 multiply_reduce_fusion.1
  230.3 17.7 %all-gather.2.cloned.1.call-done = bf16[192,3584]{1,0:T(8,128)(2,1)} async-done(((bf16[48,3584]{1,0:T(8,128)(2,1)}), bf16[192,3584]{1,0:T(8,128)(2,1)}) %all-gather.2.cloned.1.call-update) | async-done | bytes 1376272 | tf_op jit(solution)/shard_map/all_gather | solution.py:124
  247.9 4.1 %fusion.41 = f32[192,448]{1,0:T(8,128)} fusion(bf16[192,3584]{1,0:T(8,128)(2,1)} %all-gather.2.cloned.1.call-done, bf16[3584,448]{0,1:T(8,128)(2,1)} %param.23), kind=kOutput, calls=%fused_computation.75 | convolution fusion | flops 616562688 | bytes 4931584 | tf_op jit(solution)/shard_map/dot_general | solution.py:125
  252.1 6.0 %fusion.10 = f32[192,3584]{1,0:T(8,128)} fusion(bf16[448,3584]{1,0:T(8,128)(2,1)S(1)} %copy-done, bf16[192,3584]{1,0:T(8,128)(2,1)} %all-gather.2.cloned.1.call-done, bf16[3584,448]{0,1:T(8,128)(2,1)} %param.24, f32[192,448]{1,0:T(8,128)} %fusion.41), kind=kOutput, calls=%fused_computation.15 | convolution fusion | flops 1233985536 | bytes 10895360 | tf_op jit(solution)/shard_map/dot_general | solution.py:128
  258.2 35.6 %reduce-scatter.5.cloned.1.call-done = f32[48,3584]{1,0:T(8,128)} async-done(((f32[192,3584]{1,0:T(8,128)}), f32[48,3584]{1,0:T(8,128)}) %reduce-scatter.5.cloned.1.call-update) | async-done | bytes 688144 | tf_op jit(solution)/shard_map/reduce_scatter | solution.py:129
  293.8 77.4 %all-reduce.5.cloned.1.call-done = f32[48,3584]{1,0:T(8,128)} async-done(((f32[48,3584]{1,0:T(8,128)}), f32[48,3584]{1,0:T(8,128)}) %all-reduce.5.cloned.1.call-update) | async-done | bytes 688144 | tf_op jit(solution)/shard_map/psum | solution.py:130
  371.1 1.2 multiply_reduce_fusion
  372.4 1.5 add_convert_fusion
  374.7 2.0 copy.77
  (60 shorter events, 8.2 us)
Async XLA Ops:
  6.5 245.5 %copy-start = (bf16[448,3584]{1,0:T(8,128)(2,1)S(1)}, bf16[448,3584]{1,0:T(8,128)(2,1)}, u32[]{:S(2)}) copy-start(bf16[448,3584]{1,0:T(8,128)(2,1)} %param.25) | copy-start | bytes 9633796
  6.5 5.7 %copy-start.4 = (f32[3584]{0:T(1024)S(1)}, f32[3584]{0:T(1024)}, u32[]{:S(2)}) copy-start(f32[3584]{0:T(1024)} %param.26) | copy-start | bytes 43012
  6.5 142.4 %reduce-scatter.3.cloned.1.call-start = ((), (), s32[]{:S(2)}) async-start(), calls=%async_computation.2 | async-start | bytes 884736 | tf_op jit(solution)/shard_map/reduce_scatter | solution.py:116
  17.0 35.6 %copy-start.8 = (s32[48]{0:T(128)S(1)}, s32[48]{0:T(128)}, u32[]{:S(2)}) copy-start(s32[48]{0:T(128)} %param.19) | copy-start | bytes 580
  17.0 35.7 %copy-start.9 = (s32[48]{0:T(128)S(1)}, s32[48]{0:T(128)}, u32[]{:S(2)}) copy-start(s32[48]{0:T(128)} %param.20) | copy-start | bytes 580
  54.9 3.6 copy-start.7
  77.0 2.9 copy-start.2
  77.0 2.9 copy-start.3
  84.7 140.9 %all-reduce.3.cloned.1.call-start = ((), (), s32[]{:S(2)}) async-start(), calls=%async_computation.3 | async-start | bytes 1376256 | tf_op jit(solution)/shard_map/psum | solution.py:121
  149.0 77.9 %copy-start.6 = (f32[3584]{0:T(1024)S(1)}, f32[3584]{0:T(1024)}, u32[]{:S(2)}) copy-start(f32[3584]{0:T(1024)} %param.27) | copy-start | bytes 43012
  152.7 76.6 %copy-start.5 = (f32[3584]{0:T(1024)S(1)}, f32[3584]{0:T(1024)}, u32[]{:S(2)}) copy-start(f32[3584]{0:T(1024)} %param.28) | copy-start | bytes 43012
  152.7 95.2 %all-gather.2.cloned.1.call-start = ((), (), s32[]{:S(2)}) async-start(), calls=%async_computation.4 | async-start | bytes 1720320 | tf_op jit(solution)/shard_map/all_gather | solution.py:124
  228.4 0.9 copy-start.1
  230.2 63.5 %reduce-scatter.5.cloned.1.call-start = ((), (), s32[]{:S(2)}) async-start(), calls=%async_computation.5 | async-start | bytes 3440640 | tf_op jit(solution)/shard_map/reduce_scatter | solution.py:129
  258.1 113.0 %all-reduce.5.cloned.1.call-start = ((), (), s32[]{:S(2)}) async-start(), calls=%async_computation.6 | async-start | bytes 1376256 | tf_op jit(solution)/shard_map/psum | solution.py:130
Sparse Core Ops, SparseCore 0:
  84.8 64.0 reduce-scatter.2
  152.9 72.6 all-reduce.2
  230.3 17.5 all-gather.1
  258.2 35.4 reduce-scatter.4
  297.4 73.6 all-reduce.4
where the time goes:
time: 384 us; the launch traced here: 383 us
  waiting for transfers between devices  244 us (64%)
  blocking collectives  55.5 us (14%)
  local copies, waits for them, and re-layouts  36.6 us (10%)
  matrix products  22.2 us (6%)
  between operations  13.3 us (3%)
  other arithmetic  11.1 us (3%)
    psum x1, waiting for transfers between devices, body(): summed = lax.psum(summed, 'seq')  77.4 us
    psum x1, waiting for transfers between devices, body(): mixed = lax.psum(partial, 'seq')  72.8 us
    reduce_scatter x1, waiting for transfers between devices, body(): outputs = lax.psum_scatter(outputs, 'seq', scatter_dimension=1, tiled=True)  40.9 us
    reduce_scatter x1, waiting for transfers between devices, body(): summed = lax.psum_scatter(summed, 'req', scatter_dimension=0, tiled=True)  35.6 us
    all_gather x1, blocking collectives, body(): projected = lax.all_gather(local_part, 'seq', axis=1, tiled=True)  33.8 us
    psum x1, blocking collectives, body(): totals = lax.psum(jnp.sum(weights, axis=-1), 'seq').reshape(rows, H)  21.7 us
    all_gather x1, waiting for transfers between devices, body(): block_rows = lax.all_gather(feed_input, 'req', axis=0, tiled=True)  17.7 us
    unnamed x26, local copies, waits for them, and re-layouts  12.7 us
  transfers between devices with their start and end apart: 5, of which 5 were waited for; matrix products, arithmetic and copies ran while one was open for 0% of the time, Pallas kernels for 0%

commit v1 on v0

--- a/solution.py
+++ b/solution.py
@@ -127,7 +127,7 @@
     hidden = (jax.nn.gelu(gate_part, approximate=True) * up_part).astype(jnp.bfloat16)
     summed = jnp.dot(hidden, down_weight, preferred_element_type=jnp.float32)
     summed = lax.psum_scatter(summed, "req", scatter_dimension=0, tiled=True)
-    summed = lax.psum(summed, "seq")
+    summed = jnp.sum(lax.all_gather(summed, "seq"), axis=0)
     results = (middle + rms_scale(summed, gain_fourth)).astype(jnp.bfloat16)
     return results.reshape(STEPS, row_count, width)
 

time: 384 us -> 401 us (1.044)
  waiting for transfers between devices: 244 us -> 259 us
    all_gather x0 -> x1, waiting for transfers between devices: none -> 91.7 us  [body(): summed = jnp.sum(lax.all_gather(summed, 'seq'), axis=0)]
    psum x1 -> x0, waiting for transfers between devices: 77.4 us -> none  [body(): summed = lax.psum(summed, 'seq')]
where the time goes in v1:
time: 401 us
  waiting for transfers between devices  259 us (65%)
  blocking collectives  55.6 us (14%)
  local copies, waits for them, and re-layouts  35.5 us (9%)
  matrix products  22.1 us (6%)
  other arithmetic  15 us (4%)
  between operations  13.3 us (3%)
    all_gather x1, waiting for transfers between devices, body(): summed = jnp.sum(lax.all_gather(summed, 'seq'), axis=0)  91.7 us
    psum x1, waiting for transfers between devices, body(): mixed = lax.psum(partial, 'seq')  72.8 us
    reduce_scatter x1, waiting for transfers between devices, body(): outputs = lax.psum_scatter(outputs, 'seq', scatter_dimension=1, tiled=True)  40.9 us
    reduce_scatter x1, waiting for transfers between devices, body(): summed = lax.psum_scatter(summed, 'req', scatter_dimension=0, tiled=True)  35.6 us
    all_gather x1, blocking collectives, body(): projected = lax.all_gather(local_part, 'seq', axis=1, tiled=True)  33.9 us
    psum x1, blocking collectives, body(): totals = lax.psum(jnp.sum(weights, axis=-1), 'seq').reshape(rows, H)  21.7 us
    all_gather x1, waiting for transfers between devices, body(): block_rows = lax.all_gather(feed_input, 'req', axis=0, tiled=True)  17.7 us
    unnamed x26, local copies, waits for them, and re-layouts  12.7 us
  transfers between devices with their start and end apart: 5, of which 5 were waited for; matrix products, arithmetic and copies ran while one was open for 0% of the time, Pallas kernels for 0%

profile of v1, /device:TPU:0, one launch (start us, length us, event | category | flops | bytes accessed | tf_op | source)
XLA Modules:
  0.0 400.5 jit_solution(16415823163129064840)
XLA Ops:
  6.6 1.4 multiply_reduce_fusion.3
  7.9 2.0 copy.64
  10.1 2.1 reshape.160
  12.3 4.8 %convolution_convert_fusion = bf16[48,1024]{1,0:T(8,128)(2,1)S(1)} fusion(bf16[3584,1024]{1,0:T(8,128)(2,1)} %param.21, f32[48,3584]{1,0:T(8,128)} %reshape.160, f32[3584]{0:T(1024)S(1)} %copy-done.4, f32[48]{0:T(128)S(1)} %rsqrt.36), kind=kOutput, calls=%fused_computation.14 | convolution fusion | flops 352886784 | bytes 8140992 | tf_op jit(solution)/shard_map/dot_general | solution.py:85
  17.1 33.9 %all_gather.12 = bf16[48,8192]{1,0:T(8,128)(2,1)S(1)} all-gather(bf16[48,1024]{1,0:T(8,128)(2,1)S(1)} %convolution_convert_fusion), channel_id=1, replica_groups=mesh['req'=4,'seq'=8] {'seq'}, dimensions={1}, use_global_device_ids=true | all-gather | bytes 884736 | tf_op jit(solution)/shard_map/all_gather | solution.py:88
  51.8 0.9 slice_convert_fusion
  53.5 1.4 copy.84
  54.8 1.1 copy.83
  59.4 3.9 copy.69
  63.3 3.9 copy.72
  67.2 3.9 copy.65
  71.2 3.9 copy.67
  75.1 1.0 subtract_convert_fusion
  76.1 2.9 fusion.40
  79.7 1.5 copy.75
  81.2 2.6 reshape.156
  83.9 21.7 %psum.14 = f32[48,16]{0,1:T(8,128)S(1)} all-reduce(f32[48,16]{0,1:T(8,128)S(1)} %bitcast.58), channel_id=1, replica_groups=mesh['req'=4,'seq'=8] {'seq'}, use_global_device_ids=true, to_apply=%region_4.5 | all-reduce | flops 768 | bytes 6144 | tf_op jit(solution)/shard_map/psum | solution.py:109
  105.8 1.4 copy.85
  107.2 40.9 %reduce-scatter.3.cloned.1.call-done = f32[48,512]{1,0:T(8,128)} async-done(((f32[48,4096]{1,0:T(8,128)}), f32[48,512]{1,0:T(8,128)}) %reduce-scatter.3.cloned.1.call-update) | async-done | bytes 98320 | tf_op jit(solution)/shard_map/reduce_scatter | solution.py:116
  148.1 3.8 fusion.29
  152.0 72.8 %all-reduce.2.cloned.1.call-done = f32[48,3584]{1,0:T(8,128)} async-done(((f32[48,3584]{1,0:T(8,128)}), f32[48,3584]{1,0:T(8,128)}) %all-reduce.2.cloned.1.call-update) | async-done | bytes 688144 | tf_op jit(solution)/shard_map/psum | solution.py:121
  224.8 1.2 multiply_reduce_fusion.2
  226.0 1.6 multiply_reduce_fusion.1
  229.5 17.7 %all-gather.4.cloned.1.call-done = bf16[192,3584]{1,0:T(8,128)(2,1)} async-done(((bf16[48,3584]{1,0:T(8,128)(2,1)}), bf16[192,3584]{1,0:T(8,128)(2,1)}) %all-gather.4.cloned.1.call-update) | async-done | bytes 1376272 | tf_op jit(solution)/shard_map/all_gather | solution.py:124
  247.1 4.1 %fusion.41 = f32[192,448]{1,0:T(8,128)} fusion(bf16[192,3584]{1,0:T(8,128)(2,1)} %all-gather.4.cloned.1.call-done, bf16[3584,448]{0,1:T(8,128)(2,1)} %param.23), kind=kOutput, calls=%fused_computation.75 | convolution fusion | flops 616562688 | bytes 4931584 | tf_op jit(solution)/shard_map/dot_general | solution.py:125
  251.3 6.0 %fusion.10 = f32[192,3584]{1,0:T(8,128)} fusion(bf16[448,3584]{1,0:T(8,128)(2,1)S(1)} %copy-done, bf16[192,3584]{1,0:T(8,128)(2,1)} %all-gather.4.cloned.1.call-done, bf16[3584,448]{0,1:T(8,128)(2,1)} %param.24, f32[192,448]{1,0:T(8,128)} %fusion.41), kind=kOutput, calls=%fused_computation.15 | convolution fusion | flops 1233985536 | bytes 10895360 | tf_op jit(solution)/shard_map/dot_general | solution.py:128
  257.3 35.6 %reduce-scatter.5.cloned.1.call-done = f32[48,3584]{1,0:T(8,128)} async-done(((f32[192,3584]{1,0:T(8,128)}), f32[48,3584]{1,0:T(8,128)}) %reduce-scatter.5.cloned.1.call-update) | async-done | bytes 688144 | tf_op jit(solution)/shard_map/reduce_scatter | solution.py:129
  292.9 91.7 %all-gather.6.cloned.1.call-done = f32[384,3584]{1,0:T(8,128)} async-done(((f32[48,3584]{1,0:T(8,128)}), f32[384,3584]{1,0:T(8,128)}) %all-gather.6.cloned.1.call-update) | async-done | bytes 5505040 | tf_op jit(solution)/shard_map/all_gather | solution.py:130
  384.7 3.7 reduce_sum.68
  388.4 1.2 multiply_reduce_fusion
  389.7 1.5 add_convert_fusion
  392.0 2.0 copy.77
  (61 shorter events, 8.8 us)
Async XLA Ops:
  6.5 244.7 %copy-start = (bf16[448,3584]{1,0:T(8,128)(2,1)S(1)}, bf16[448,3584]{1,0:T(8,128)(2,1)}, u32[]{:S(2)}) copy-start(bf16[448,3584]{1,0:T(8,128)(2,1)} %param.25) | copy-start | bytes 9633796
  6.5 5.7 %copy-start.4 = (f32[3584]{0:T(1024)S(1)}, f32[3584]{0:T(1024)}, u32[]{:S(2)}) copy-start(f32[3584]{0:T(1024)} %param.26) | copy-start | bytes 43012
  6.5 141.6 %reduce-scatter.3.cloned.1.call-start = ((), (), s32[]{:S(2)}) async-start(), calls=%async_computation.2 | async-start | bytes 884736 | tf_op jit(solution)/shard_map/reduce_scatter | solution.py:116
  17.0 35.7 %copy-start.8 = (s32[48]{0:T(128)S(1)}, s32[48]{0:T(128)}, u32[]{:S(2)}) copy-start(s32[48]{0:T(128)} %param.19) | copy-start | bytes 580
  17.0 35.8 %copy-start.9 = (s32[48]{0:T(128)S(1)}, s32[48]{0:T(128)}, u32[]{:S(2)}) copy-start(s32[48]{0:T(128)} %param.20) | copy-start | bytes 580
  17.0 36.3 %copy-start.7 = (s32[1,512]{1,0:T(1,128)S(1)}, s32[1,512]{1,0:T(1,128)}, u32[]{:S(2)}) copy-start(s32[1,512]{1,0:T(1,128)} %param.18) | copy-start | bytes 6148
  76.1 2.9 copy-start.2
  76.1 2.9 copy-start.3
  83.8 140.9 %all-reduce.2.cloned.1.call-start = ((), (), s32[]{:S(2)}) async-start(), calls=%async_computation.3 | async-start | bytes 1376256 | tf_op jit(solution)/shard_map/psum | solution.py:121
  148.1 77.9 %copy-start.6 = (f32[3584]{0:T(1024)S(1)}, f32[3584]{0:T(1024)}, u32[]{:S(2)}) copy-start(f32[3584]{0:T(1024)} %param.27) | copy-start | bytes 43012
  151.9 76.6 %copy-start.5 = (f32[3584]{0:T(1024)S(1)}, f32[3584]{0:T(1024)}, u32[]{:S(2)}) copy-start(f32[3584]{0:T(1024)} %param.28) | copy-start | bytes 43012
  151.9 95.2 %all-gather.4.cloned.1.call-start = ((), (), s32[]{:S(2)}) async-start(), calls=%async_computation.4 | async-start | bytes 1720320 | tf_op jit(solution)/shard_map/all_gather | solution.py:124
  227.6 0.9 copy-start.1
  229.4 63.5 %reduce-scatter.5.cloned.1.call-start = ((), (), s32[]{:S(2)}) async-start(), calls=%async_computation.5 | async-start | bytes 3440640 | tf_op jit(solution)/shard_map/reduce_scatter | solution.py:129
  257.3 127.4 %all-gather.6.cloned.1.call-start = ((), (), s32[]{:S(2)}) async-start(), calls=%async_computation.6 | async-start | bytes 6193152 | tf_op jit(solution)/shard_map/all_gather | solution.py:130
Sparse Core Ops, SparseCore 0:
  84.0 64.1 reduce-scatter.2
  152.0 72.6 all-reduce.1
  229.5 17.5 all-gather.3
  257.4 35.4 reduce-scatter.4
  295.2 89.4 all-gather.5
